TPU v7x, 128 devices: a whole 4x4x4 slice. The times are simulated.
128 devices in a mesh: gx: 4 (over x), gy: 4 (over z), gz: 8 (over y, core).
Axes of the slice: x: 4, y: 4, z: 4, core: 2. Of those that a mesh axis runs over, the one named last changes fastest.
Arguments:
- element_load: float32 [36, 36, 72, 128], P('gx', 'gy', 'gz'), may hold values from -90 to 90
- local_matrix: float32 [4, 4, 8, 729, 729], P('gx', 'gy', 'gz'), may hold values from -10 to 61, as said below
- dirichlet_inverse: float32 [4, 4, 8, 343, 343], P('gx', 'gy', 'gz'), as said below
- neumann_inverse: float32 [4, 4, 8, 729, 729], P('gx', 'gy', 'gz'), as said below
- coarse_basis: float32 [4, 4, 8, 20, 729], P('gx', 'gy', 'gz'), as said below
Outputs:
- solution: float32 [36, 36, 72, 128], P('gx', 'gy', 'gz')
- residual: float32 [36, 36, 72, 128], P('gx', 'gy', 'gz')
Inputs may be any that keep to these rules, and one draw needn't show every extreme that they name: `local_matrix`: block (a, b, c) is the symmetric positive definite stiffness matrix of subdomain (a, b, c) in the node order of the steps: cellwise conductivities on the couplings of neighbouring nodes plus a lumped reaction term. `dirichlet_inverse`: block (a, b, c) is the inverse, computed in float32, of local_matrix's block restricted to the inner nodes. `neumann_inverse`: block (a, b, c) is the node-by-node block of the inverse, computed in float32, of the saddle-point matrix [[A, Cm^T], [Cm, 0]], with A local_matrix's block and Cm the 20 x 729 primal constraints in the order of the coarse numbering: the value at each of the 8 corners, then the mean over the 7 inner nodes of each of the 12 edges. `coarse_basis`: block (a, b, c) is the constraint-by-node block of that same saddle-point inverse.
All inputs are finite; a program needn't handle non-finite values.
Results may differ from a plain program's by a relative error of at most 0.0014.
Values sent between devices are 32-bit elements; how exact they have to be, the bound alone decides.
A program may use at most 128 MiB of HBM per device.

v0:
```python
import functools

import jax
import jax.numpy as jnp
from jax import lax
from jax.sharding import Mesh
from jax.sharding import PartitionSpec as P

ITERS = 2
GZ = ("gz_0", "gz_1")
GX_GY_GZ = ("gx", "gy", "gz_0", "gz_1")


def with_halo(array, sides, width):
    for axis, dim in sides:
        size, length = (lax.axis_size(axis), array.shape[dim])
        up = [(i, (i + 1) % size) for i in range(size)]
        down = [(j, i) for i, j in up]
        last = lax.slice_in_dim(array, length - width, length, axis=dim)
        leading = lax.slice_in_dim(array, 0, width, axis=dim)
        before = lax.ppermute(last, axis, up)
        after = lax.ppermute(leading, axis, down)
        array = jnp.concatenate([before, array, after], axis=dim)
    return array


def over_axes(array, axes):
    return functools.reduce(lax.psum, axes, array)


def matmul(left_side, right_side):
    return jnp.dot(
        left_side, right_side, precision=lax.Precision.HIGHEST, preferred_element_type=jnp.float32
    )


def coarse_ids(along_x, along_y, along_z, count_x, count_y, count_z):
    total = count_x * count_y * count_z

    def vertex(shift_x, shift_y, shift_z):
        return (
            (along_x + shift_x) % count_x * count_y + (along_y + shift_y) % count_y
        ) * count_z + (along_z + shift_z) % count_z

    listed = [vertex(sx, sy, sz) for sx in (0, 1) for sy in (0, 1) for sz in (0, 1)]
    listed += [total + vertex(0, sy, sz) for sy in (0, 1) for sz in (0, 1)]
    listed += [2 * total + vertex(sx, 0, sz) for sx in (0, 1) for sz in (0, 1)]
    listed += [3 * total + vertex(sx, sy, 0) for sx in (0, 1) for sy in (0, 1)]
    return jnp.stack(listed, axis=-1)


def node_weights(node_side):
    places = jnp.arange(node_side, dtype=jnp.int32)
    on_rim = ((places == 0) | (places == node_side - 1)).astype(jnp.int32)
    rims = on_rim[:, None, None] + on_rim[None, :, None] + on_rim[None, None, :]
    copies = (
        (1.0 + on_rim[:, None, None].astype(jnp.float32))
        * (1.0 + on_rim[None, :, None].astype(jnp.float32))
        * (1.0 + on_rim[None, None, :].astype(jnp.float32))
    )
    share = (1.0 / copies)[..., None]
    border = jnp.where(rims[..., None] > 0, share, jnp.zeros_like(share))
    return (share, border)


def fold_rim(padded, axis_dim):
    length = padded.shape[axis_dim]
    inside = lax.slice_in_dim(padded, 1, length - 1, axis=axis_dim)
    lowest = lax.slice_in_dim(padded, 0, 1, axis=axis_dim)
    highest = lax.slice_in_dim(padded, length - 1, length, axis=axis_dim)
    middle_shape = list(lowest.shape)
    middle_shape[axis_dim] = length - 4
    addend = jnp.concatenate(
        [lowest, jnp.zeros(middle_shape, padded.dtype), highest], axis=axis_dim
    )
    return inside + addend


def local(element_load, local_matrix, dirichlet_inverse, neumann_inverse, coarse_basis):
    highest_prec = lax.Precision.HIGHEST
    node_side = element_load.shape[0]
    rhs_count = element_load.shape[3]
    node_count = node_side**3
    inner_side = node_side - 2
    inner_count = inner_side**3
    primal = coarse_basis.shape[3]
    stiffness = local_matrix.reshape(node_count, node_count)
    interior_inverse = dirichlet_inverse.reshape(inner_count, inner_count)
    neumann = neumann_inverse.reshape(node_count, node_count)
    basis = coarse_basis.reshape(primal, node_count)
    stiff_cols = stiffness.reshape(node_count, node_side, node_side, node_side)[
        :, 1:-1, 1:-1, 1:-1
    ].reshape(node_count, inner_count)
    stiff_rows = stiffness.reshape(node_side, node_side, node_side, node_count)[
        1:-1, 1:-1, 1:-1
    ].reshape(inner_count, node_count)
    share, border = node_weights(node_side)
    count_x = lax.axis_size("gx")
    count_y = lax.axis_size("gy")
    count_z = lax.axis_size(GZ)
    coarse_count = 4 * count_x * count_y * count_z
    own_ids = coarse_ids(
        lax.axis_index("gx"), lax.axis_index("gy"), lax.axis_index(GZ), count_x, count_y, count_z
    )
    columns = jnp.arange(coarse_count, dtype=jnp.int32)
    own_indicator = (own_ids[:, None] == columns[None, :]).astype(jnp.float32)
    coarse_local = matmul(basis, matmul(stiffness, basis.T))

    def piece_indicator(count_rows):
        linear = jnp.arange(count_rows, dtype=jnp.int32)
        piece_ids = coarse_ids(
            linear // (count_y * count_z),
            linear // count_z % count_y,
            linear % count_z,
            count_x,
            count_y,
            count_z,
        )
        return (piece_ids[:, :, None] == columns[None, None, :]).astype(jnp.float32)

    received = lax.all_gather(coarse_local[None], GX_GY_GZ, axis=0, tiled=True)
    indicator = piece_indicator(received.shape[0])
    partial_rows = jnp.einsum("zpm,zpq->zmq", indicator, received, precision=highest_prec)
    coarse_matrix = jnp.einsum("zmq,zqn->mn", partial_rows, indicator, precision=highest_prec)
    factor = jnp.linalg.cholesky(coarse_matrix)

    def coarse_rhs(primal_load):
        received = lax.all_gather(primal_load[None], GX_GY_GZ, axis=0, tiled=True)
        indicator = piece_indicator(received.shape[0])
        return jnp.einsum("zpm,zpk->mk", indicator, received, precision=highest_prec)

    def assemble(field):
        padded = with_halo(field, (("gx", 0), ("gy", 1), (GZ, 2)), 1)
        result_field = fold_rim(fold_rim(fold_rim(padded, 0), 1), 2)
        return result_field

    cube_shape = (node_side, node_side, node_side, rhs_count)

    def apply_operator(field):
        return assemble(matmul(stiffness, field.reshape(node_count, rhs_count)).reshape(cube_shape))

    def precondition(current):
        inner_part = current[1:-1, 1:-1, 1:-1].reshape(inner_count, rhs_count)
        start = matmul(interior_inverse, inner_part)
        spill = matmul(stiff_cols, start).reshape(cube_shape)
        first_residual = current - assemble(spill)
        weighted = (border * first_residual).reshape(node_count, rhs_count)
        local_part = matmul(neumann, weighted)
        primal_load = matmul(basis, weighted)
        coarse_values = jax.scipy.linalg.cho_solve((factor, True), coarse_rhs(primal_load))
        primal_values = matmul(own_indicator, coarse_values)
        combined = local_part + matmul(basis.T, primal_values)
        surface = assemble(border * combined.reshape(cube_shape))
        inner_new = start - matmul(
            interior_inverse, matmul(stiff_rows, surface.reshape(node_count, rhs_count))
        )
        padded_inner = jnp.pad(
            inner_new.reshape(inner_side, inner_side, inner_side, rhs_count),
            ((1, 1), (1, 1), (1, 1), (0, 0)),
        )
        return surface + padded_inner

    right_side = assemble(element_load)
    solution = jnp.zeros(cube_shape, jnp.float32)
    residual = right_side

    def both_dots(resid_now, precond_now, mapped_now):
        return (
            over_axes(jnp.sum(resid_now * precond_now * share, axis=(0, 1, 2)), GX_GY_GZ),
            over_axes(jnp.sum(precond_now * mapped_now * share, axis=(0, 1, 2)), GX_GY_GZ),
        )

    precond_now = precondition(residual)
    mapped_now = apply_operator(precond_now)
    gamma_old, delta_now = both_dots(residual, precond_now, mapped_now)
    step_size = gamma_old / delta_now
    direction = precond_now
    image_dir = mapped_now
    for iteration in range(ITERS):
        solution = solution + step_size * direction
        residual = residual - step_size * image_dir
        if iteration + 1 < ITERS:
            precond_now = precondition(residual)
            mapped_now = apply_operator(precond_now)
            gamma_new, delta_now = both_dots(residual, precond_now, mapped_now)
            scaling = gamma_new / gamma_old
            step_size = gamma_new / (delta_now - scaling * gamma_new / step_size)
            direction = precond_now + scaling * direction
            image_dir = mapped_now + scaling * image_dir
            gamma_old = gamma_new
    return (solution, residual)


def solution(mesh):
    split = Mesh(
        mesh.devices.reshape(mesh.shape["gx"], mesh.shape["gy"], 4, 2), ("gx", "gy", "gz_0", "gz_1")
    )
    return jax.shard_map(
        local,
        mesh=split,
        in_specs=(
            P("gx", "gy", GZ, None),
            P("gx", "gy", GZ, None, None),
            P("gx", "gy", GZ, None, None),
            P("gx", "gy", GZ, None, None),
            P("gx", "gy", GZ, None, None),
        ),
        out_specs=(P("gx", "gy", GZ, None), P("gx", "gy", GZ, None)),
        check_vma=False,
    )
```

profile of v0, /device:TPU:1, one launch (start us, length us, event | category | flops | bytes accessed | tf_op | source)
XLA Modules:
  0.0 601.1 jit_solution(7380136900972407023)
XLA Ops:
  13.8 3.3 copy.18
  17.2 2.9 fusion.11
  20.4 40.2 %all-gather.3 = f32[128,20,20]{2,1,0:T(8,128)S(1)} all-gather(f32[1,20,20]{2,1,0:T(8,128)S(1)} %copy.17), channel_id=2, replica_groups=mesh['gx'=4,'gy'=4,'gz_0'=4,'gz_1'=2] {'gx','gy','gz_0','gz_1'}, dimensions={0}, use_global_device_ids=true | all-gather | bytes 206400 | tf_op jit(solution)/shard_map/all_gather | solution.py:121
  60.6 3.8 fusion.247
  64.5 10.9 %fusion.22 = f32[512,512]{1,0:T(8,128)S(1)} fusion(s32[128,20]{0,1:T(8,128)S(1)} %copy-done.55, f32[128,512,20]{1,2,0:T(8,128)S(1)} %fusion.247), kind=kOutput, calls=%fused_computation.25 | convolution fusion | flops 8054374400 | bytes 6301696 | tf_op jit(solution)/shard_map/zmq,zqn->mn/dot_general | solution.py:124
  79.2 11.7 %cholesky.106 = f32[128,128]{1,0:T(8,128)S(1)} custom-call(f32[128,128]{1,0:T(8,128)S(1)} %cholesky.269), custom_call_target="Cholesky" | custom-call | tf_op jit(solution)/shard_map/jit(cholesky)/cholesky | solution.py:125
  91.5 9.8 %custom-call.32 = f32[1,128,128]{1,2,0:T(8,128)S(1)} custom-call(f32[1,128,128]{2,1,0:T(8,128)S(1)} %get-tuple-element.130), custom_call_target="InvertDiagBlocksLowerTriangular" | custom-call | tf_op jit(solution)/shard_map/jit(cholesky)/cholesky | solution.py:125
  105.0 11.7 %cholesky.220 = f32[128,128]{1,0:T(8,128)S(1)} custom-call(f32[128,128]{1,0:T(8,128)S(1)} %cholesky.273), custom_call_target="Cholesky" | custom-call | tf_op jit(solution)/shard_map/jit(cholesky)/cholesky | solution.py:125
  117.3 9.8 %custom-call.33 = f32[1,128,128]{1,2,0:T(8,128)S(1)} custom-call(f32[1,128,128]{2,1,0:T(8,128)S(1)} %get-tuple-element.127), custom_call_target="InvertDiagBlocksLowerTriangular" | custom-call | tf_op jit(solution)/shard_map/jit(cholesky)/cholesky | solution.py:125
  130.2 13.2 %cholesky.241 = f32[128,128]{1,0:T(8,128)} custom-call(f32[128,128]{1,0:T(8,128)} %cholesky.278), custom_call_target="Cholesky" | custom-call | tf_op jit(solution)/shard_map/jit(cholesky)/cholesky | solution.py:125
  145.4 11.4 %custom-call.34 = f32[1,128,128]{1,2,0:T(8,128)} custom-call(f32[1,128,128]{2,1,0:T(8,128)} %get-tuple-element.124), custom_call_target="InvertDiagBlocksLowerTriangular" | custom-call | tf_op jit(solution)/shard_map/jit(cholesky)/cholesky | solution.py:125
  165.6 5.0 copy.16
  170.6 3.7 reshape_reshape.6
  190.0 3.3 convolution_bitcast_fusion.1
  200.7 2.7 collective-permute-start.9
  204.1 12.6 %cholesky.258 = f32[128,128]{1,0:T(8,128)S(1)} custom-call(f32[128,128]{1,0:T(8,128)} %convolution_subtract_fusion.16), custom_call_target="Cholesky" | custom-call | tf_op jit(solution)/shard_map/jit(cholesky)/cholesky | solution.py:125
  234.9 10.1 %while.4 = (s32[]{:T(128)}, f32[512,512]{1,0:T(8,128)S(1)}, s32[4,2]{0,1:T(2,128)S(1)}, f32[4,128,128]{2,1,0:T(8,128)}, s32[]{:T(128)}) while((s32[]{:T(128)}, f32[512,512]{1,0:T(8,128)S(1)}, s32[4,2]{0,1:T(2,128)S(1)}, f32[4,128,128]{2,1,0:T(8,128)}, s32[]{:T(128)}) %tuple.85), condition=%wide.while_cond, body=%wide.while_body.sunk | while | flops 2 | bytes 132705 | solution.py:150
  245.0 40.2 %custom-call.36 = f32[4,128,128]{1,2,0:T(8,128)S(1)} custom-call(f32[4,128,128]{2,1,0:T(8,128)} %get-tuple-element.17), custom_call_target="InvertDiagBlocksLowerTriangular" | custom-call | tf_op jit(solution)/shard_map/jit(_cho_solve)/triangular_solve | solution.py:150
  285.9 4.4 fusion.15
  290.3 4.0 all-gather.9.cloned.1.call-done
  294.3 4.1 fusion.35
  305.8 2.7 collective-permute-start.13
  310.6 2.8 collective-permute-start.15
  317.6 7.4 %reduce.24 = f32[729,729]{1,0:T(8,128)} reduce(f32[1,1,1,729,729]{4,2,3,1,0:T(1,128)S(1)} %copy-done, f32[]{:T(128)} %constant.1059), dimensions={0,1,2}, to_apply=%param.8.reduce_sub_computation | reduce | bytes 4251532 | tf_op args[1]
  325.0 3.7 reshape_reshape.7
  342.9 2.9 fusion.27
  346.5 2.7 collective-permute-start.19
  351.3 2.9 collective-permute-start.21
  356.1 3.3 collective-permute-start.22
  365.5 9.2 %all-reduce.8 = (f32[128]{0:T(128)S(1)}, f32[128]{0:T(128)S(1)}) all-reduce(f32[128]{0:T(128)S(1)} %get-tuple-element.22, f32[128]{0:T(128)S(1)} %get-tuple-element.21), channel_id=1, replica_groups=mesh['gx'=4,'gy'=4,'gz_0'=4,'gz_1'=2] {'gx'}, use_global_device_ids=true, to_apply=%region_9.11 | all-reduce | flops 256 | bytes 2048 | tf_op jit(solution)/shard_map/psum | solution.py:28
  374.7 9.0 %all-reduce.6 = (f32[128]{0:T(128)S(1)}, f32[128]{0:T(128)S(1)}) all-reduce(f32[128]{0:T(128)S(1)} %get-tuple-element.41, f32[128]{0:T(128)S(1)} %get-tuple-element.42), channel_id=1, replica_groups=mesh['gx'=4,'gy'=4,'gz_0'=4,'gz_1'=2] {'gy'}, use_global_device_ids=true, to_apply=%region_10.12 | all-reduce | flops 256 | bytes 2048 | tf_op jit(solution)/shard_map/psum | solution.py:28
  383.7 11.0 %all-reduce.4 = (f32[128]{0:T(128)S(1)}, f32[128]{0:T(128)S(1)}) all-reduce(f32[128]{0:T(128)S(1)} %get-tuple-element.37, f32[128]{0:T(128)S(1)} %get-tuple-element.38), channel_id=1, replica_groups=mesh['gx'=4,'gy'=4,'gz_0'=4,'gz_1'=2] {'gz_0'}, use_global_device_ids=true, to_apply=%region_11.13 | all-reduce | flops 256 | bytes 2048 | tf_op jit(solution)/shard_map/psum | solution.py:28
  394.7 5.3 all-reduce.10
  409.3 2.7 collective-permute-start.25
  413.6 3.0 collective-permute-start.27
  418.3 4.2 collective-permute-start.28
  430.9 4.3 fusion.13
  435.2 61.6 %all-gather.11.cloned.1.call-done = f32[128,20,128]{2,1,0:T(8,128)} async-done(((f32[1,20,128]{2,1,0:T(8,128)}), f32[128,20,128]{2,1,0:T(8,128)}) %all-gather.11.cloned.1.call-update) | async-done | bytes 1310736 | tf_op jit(solution)/shard_map/all_gather | solution.py:128
  496.8 4.1 fusion.38
  508.3 2.7 collective-permute-start.31
  513.1 2.8 collective-permute-start.33
  536.6 2.9 fusion.30
  549.6 2.7 collective-permute-start.40
  557.8 9.0 %all-reduce.7 = (f32[128]{0:T(128)S(1)}, f32[128]{0:T(128)S(1)}) all-reduce(f32[128]{0:T(128)S(1)} %get-tuple-element.20, f32[128]{0:T(128)S(1)} %get-tuple-element.19), channel_id=1, replica_groups=mesh['gx'=4,'gy'=4,'gz_0'=4,'gz_1'=2] {'gx'}, use_global_device_ids=true, to_apply=%region_19.21 | all-reduce | flops 256 | bytes 2048 | tf_op jit(solution)/shard_map/psum | solution.py:28
  566.8 8.7 %all-reduce.5 = (f32[128]{0:T(128)S(1)}, f32[128]{0:T(128)S(1)}) all-reduce(f32[128]{0:T(128)S(1)} %get-tuple-element.39, f32[128]{0:T(128)S(1)} %get-tuple-element.40), channel_id=1, replica_groups=mesh['gx'=4,'gy'=4,'gz_0'=4,'gz_1'=2] {'gy'}, use_global_device_ids=true, to_apply=%region_20.22 | all-reduce | flops 256 | bytes 2048 | tf_op jit(solution)/shard_map/psum | solution.py:28
  575.5 10.6 %all-reduce.3 = (f32[128]{0:T(128)S(1)}, f32[128]{0:T(128)S(1)}) all-reduce(f32[128]{0:T(128)S(1)} %get-tuple-element.35, f32[128]{0:T(128)S(1)} %get-tuple-element.36), channel_id=1, replica_groups=mesh['gx'=4,'gy'=4,'gz_0'=4,'gz_1'=2] {'gz_0'}, use_global_device_ids=true, to_apply=%region_21.23 | all-reduce | flops 256 | bytes 2048 | tf_op jit(solution)/shard_map/psum | solution.py:28
  586.1 5.3 all-reduce.9
  591.4 2.7 multiply_subtract_fusion
  (424 shorter events, 183.6 us)
Async XLA Ops:
  7.2 287.1 %all-gather.9.cloned.1.call-start = ((), (), s32[]{:S(2)}) async-start(), calls=%async_computation | async-start | bytes 1585152 | tf_op jit(solution)/shard_map/all_gather | solution.py:128
  8.8 151.1 %collective-permute-start = (f32[1,9,9,128]{3,2,1,0:T(8,128)}, f32[1,9,9,128]{3,2,1,0:T(8,128)}, u32[]{:S(2)}, u32[]{:S(2)}) collective-permute-start(f32[1,9,9,128]{3,2,1,0:T(8,128)} %get-tuple-element.112), channel_id=1, source_target_pairs={{0,32},{32,64},{64,96},{96,0},{1,33},{33,65},{65,97},{97,1},{2,34}... | collective-permute-start | bytes 124424 | tf_op jit(solution)/shard_map/ppermute | solution.py:21
  10.8 151.1 %collective-permute-start.1 = (f32[1,9,9,128]{3,2,1,0:T(8,128)}, f32[1,9,9,128]{3,2,1,0:T(8,128)}, u32[]{:S(2)}, u32[]{:S(2)}) collective-permute-start(f32[1,9,9,128]{3,2,1,0:T(8,128)} %get-tuple-element.111), channel_id=1, source_target_pairs={{32,0},{64,32},{96,64},{0,96},{33,1},{65,33},{97,65},{1,97},{34,2}... | collective-permute-start | bytes 124424 | tf_op jit(solution)/shard_map/ppermute | solution.py:22
  20.4 40.2 %copy-start.24 = (pred[128,20,512]{2,1,0:T(8,128)(4,1)S(1)}, pred[128,20,512]{2,1,0:T(8,128)(4,1)}, u32[]{:S(2)}) copy-start(pred[128,20,512]{2,1,0:T(8,128)(4,1)} %copy.18) | copy-start | bytes 3932164
  162.8 16.5 %collective-permute-start.2 = (f32[11,1,9,128]{3,2,1,0:T(8,128)S(1)}, f32[11,1,9,128]{3,2,1,0:T(8,128)S(1)}, u32[]{:S(2)}, u32[]{:S(2)}) collective-permute-start(f32[11,1,9,128]{3,2,1,0:T(8,128)S(1)} %get-tuple-element.91), channel_id=1, source_target_pairs={{0,8},{8,16},{16,24},{24,0},{1,9},{9,17},{17,25},{25,1},{2,10},{10... | collective-permute-start | bytes 152072 | tf_op jit(solution)/shard_map/ppermute | solution.py:21
  162.9 16.4 %collective-permute-start.3 = (f32[11,1,9,128]{3,2,1,0:T(8,128)S(1)}, f32[11,1,9,128]{3,2,1,0:T(8,128)S(1)}, u32[]{:S(2)}, u32[]{:S(2)}) collective-permute-start(f32[11,1,9,128]{3,2,1,0:T(8,128)S(1)} %get-tuple-element.92), channel_id=1, source_target_pairs={{8,0},{16,8},{24,16},{0,24},{9,1},{17,9},{25,17},{1,25},{10,2},{18... | collective-permute-start | bytes 152072 | tf_op jit(solution)/shard_map/ppermute | solution.py:22
  179.4 2.0 collective-permute-start.4
  180.1 3.9 collective-permute-start.5
  193.9 4.6 collective-permute-start.6
  195.8 3.9 collective-permute-start.7
  200.7 16.1 %collective-permute-start.8 = (f32[11,1,9,128]{3,2,1,0:T(8,128)S(1)}, f32[11,1,9,128]{3,2,1,0:T(8,128)S(1)}, u32[]{:S(2)}, u32[]{:S(2)}) collective-permute-start(f32[11,1,9,128]{3,2,1,0:T(8,128)S(1)} %get-tuple-element.87), channel_id=1, source_target_pairs={{0,8},{8,16},{16,24},{24,0},{1,9},{9,17},{17,25},{25,1},{2,10},{10... | collective-permute-start | bytes 152072 | tf_op jit(solution)/shard_map/ppermute | solution.py:21
  200.7 16.0 %collective-permute-start.9 = (f32[11,1,9,128]{3,2,1,0:T(8,128)S(1)}, f32[11,1,9,128]{3,2,1,0:T(8,128)S(1)}, u32[]{:S(2)}, u32[]{:S(2)}) collective-permute-start(f32[11,1,9,128]{3,2,1,0:T(8,128)S(1)} %get-tuple-element.88), channel_id=1, source_target_pairs={{8,0},{16,8},{24,16},{0,24},{9,1},{17,9},{25,17},{1,25},{10,2},{18... | collective-permute-start | bytes 152072 | tf_op jit(solution)/shard_map/ppermute | solution.py:22
  218.0 3.4 collective-permute-start.10
  219.9 3.7 collective-permute-start.11
  228.1 268.7 %all-gather.11.cloned.1.call-start = ((), (), s32[]{:S(2)}) async-start(), calls=%async_computation.1 | async-start | bytes 1585152 | tf_op jit(solution)/shard_map/all_gather | solution.py:128
  245.0 56.7 %copy-start.18 = (f32[512,512]{1,0:T(8,128)}, f32[512,512]{1,0:T(8,128)S(1)}, u32[]{:S(2)}) copy-start(f32[512,512]{1,0:T(8,128)S(1)} %get-tuple-element.203) | copy-start | bytes 3145732
  305.7 4.8 collective-permute-start.12
  305.8 4.7 collective-permute-start.13
  310.5 4.7 collective-permute-start.14
  310.6 4.6 collective-permute-start.15
  315.3 18.3 %collective-permute-start.16 = (f32[11,11,1,128]{3,2,1,0:T(1,128)S(1)}, f32[11,11,1,128]{3,2,1,0:T(1,128)S(1)}, u32[]{:S(2)}, u32[]{:S(2)}) collective-permute-start(f32[11,11,1,128]{3,2,1,0:T(1,128)S(1)} %get-tuple-element.59), channel_id=1, source_target_pairs={{0,1},{1,2},{2,3},{3,4},{4,5},{5,6},{6,7},{7,0},{8,9},{9,10},{10,1... | collective-permute-start | bytes 185864 | tf_op jit(solution)/shard_map/ppermute | solution.py:21
  317.4 16.2 %collective-permute-start.17 = (f32[11,11,1,128]{3,2,1,0:T(1,128)S(1)}, f32[11,11,1,128]{3,2,1,0:T(1,128)S(1)}, u32[]{:S(2)}, u32[]{:S(2)}) collective-permute-start(f32[11,11,1,128]{3,2,1,0:T(1,128)S(1)} %get-tuple-element.60), channel_id=1, source_target_pairs={{1,0},{2,1},{3,2},{4,3},{5,4},{6,5},{7,6},{0,7},{9,8},{10,9},{11,1... | collective-permute-start | bytes 185864 | tf_op jit(solution)/shard_map/ppermute | solution.py:22
  345.9 4.9 collective-permute-start.18
  346.5 4.4 collective-permute-start.19
  350.9 5.1 collective-permute-start.20
  351.3 4.7 collective-permute-start.21
  356.1 5.5 collective-permute-start.22
  359.4 3.7 collective-permute-start.23
  408.2 4.5 collective-permute-start.24
  409.3 4.1 collective-permute-start.25
  413.5 4.7 collective-permute-start.26
  413.6 4.6 collective-permute-start.27
  418.3 5.5 collective-permute-start.28
  422.5 3.7 collective-permute-start.29
  430.8 65.9 %copy-start.56 = (s32[128,20]{0,1:T(8,128)S(1)}, s32[128,20]{0,1:T(8,128)}, u32[]{:S(2)}) copy-start(s32[128,20]{0,1:T(8,128)} %copy-done.54) | copy-start | bytes 30724
  435.2 65.7 %copy-start.26 = (f32[4,128,128]{1,2,0:T(8,128)S(1)}, f32[4,128,128]{1,2,0:T(8,128)}, u32[]{:S(2)}) copy-start(f32[4,128,128]{1,2,0:T(8,128)} %copy-done.25) | copy-start | bytes 786436
  508.2 4.8 collective-permute-start.30
  508.3 4.7 collective-permute-start.31
  513.1 4.7 collective-permute-start.32
  513.1 4.6 collective-permute-start.33
  517.8 3.4 collective-permute-start.34
  519.9 3.7 collective-permute-start.35
  539.6 4.7 collective-permute-start.36
  540.6 3.8 collective-permute-start.37
  544.4 5.1 collective-permute-start.38
  545.4 4.1 collective-permute-start.39
  549.6 4.0 collective-permute-start.40
  552.3 3.7 collective-permute-start.41
  (63 other events, 475.7 us)
Sparse Core Ops, SparseCore 0:
  228.2 66.0 all-gather.8
  431.0 65.7 all-gather.10
where the time goes:
time: 607 us; the launch traced here: 601 us
  other arithmetic  161 us (27%)
  blocking collectives  108 us (18%)
  waiting for transfers between devices  101 us (17%)
  matrix products  76 us (13%)
  local copies, waits for them, and re-layouts  74.1 us (12%)
  starting transfers between devices  62.3 us (10%)
  between operations  18.4 us (3%)
    another operation x15, other arithmetic, local(): factor = jnp.linalg.cholesky(coarse_matrix)  86.6 us
    psum x8, blocking collectives, over_axes(): return functools.reduce(lax.psum, axes, array)  68.1 us
    all_gather x2, waiting for transfers between devices, coarse_rhs(): received = lax.all_gather(primal_load[None], GX_GY_GZ, axis=0, tiled=True)  65.6 us
    another operation x4, other arithmetic, precondition(): jax.scipy.linalg.cho_solve((factor, True), coarse_rhs(primal_load))  41.5 us
    all_gather x1, blocking collectives, local(): received = lax.all_gather(coarse_local[None], GX_GY_GZ, axis=0, tiled=True)  40.2 us
    ppermute x21, starting transfers between devices, with_halo(): after = lax.ppermute(leading, axis, down)  39.1 us
    dot_general x20, matrix products, matmul(): jnp.dot(left_side, right_side, precision=lax.Precision.HIGHEST, preferred...  36.9 us
    ppermute x21, starting transfers between devices, with_halo(): before = lax.ppermute(last, axis, up)  22.7 us
  transfers between devices with their start and end apart: 44, of which 26 were waited for; matrix products, arithmetic and copies ran while one was open for 36% of the time, Pallas kernels for 0%

commit v1 on v0

v1 whole, which is shorter than its diff:
```python
import functools

import jax
import jax.numpy as jnp
import numpy as np
from jax import lax
from jax.experimental import pallas as pl
from jax.experimental.pallas import tpu as pltpu
from jax.sharding import PartitionSpec as P

MESH = pl.DeviceIdType.MESH
F32, BF16 = jnp.float32, jnp.bfloat16
GX, GY, GZ = 4, 4, 8
M = 9
NODES, NB, NI, RHS = 729, 392, 343, 128
ORDER = (1, 3, 5, 7, 2, 6, 0, 4)
VM = pl.BlockSpec(memory_space=pltpu.VMEM)

_g = np.indices((M, M, M)).reshape(3, -1)
_rim = ((_g == 0) | (_g == M - 1)).sum(0)
B_IDS, I_IDS = np.where(_rim > 0)[0], np.where(_rim == 0)[0]
B_POS = {int(n): r for r, n in enumerate(B_IDS)}


def one_hot(rows, cols, shape):
    out = np.zeros(shape, np.float32)
    out[rows, cols] = 1.0
    return out


PB = one_hot(np.arange(len(B_IDS)), B_IDS, (NB, NODES))
PI = one_hot(np.arange(NI), I_IDS, (NI, NODES))
WEIGHT = np.zeros((NB, 1), np.float32)
WEIGHT[: len(B_IDS), 0] = 1.0 / 2.0 ** _rim[B_IDS]
WEIGHT = np.broadcast_to(WEIGHT, (NB, RHS)).copy()

DIRS = sorted(
    ((x, y, z) for x in (-1, 0, 1) for y in (-1, 0, 1) for z in (-1, 0, 1) if (x, y, z) != (0, 0, 0)),
    key=lambda d: (sum(map(abs, d)), d),
)
SIZE = {1: 88, 2: 16, 3: 8}
OFFS, _at = {}, 0
for _d in DIRS:
    OFFS[_d] = (_at, SIZE[sum(map(abs, _d))])
    _at += OFFS[_d][1]
NS = _at
PK = np.zeros((NS, NB), np.float32)
for _d in DIRS:
    _sel = [[0] if v == -1 else [M - 1] if v == 1 else list(range(M)) for v in _d]
    for _r, (_i, _j, _k) in enumerate((i, j, k) for i in _sel[0] for j in _sel[1] for k in _sel[2]):
        PK[OFFS[_d][0] + _r, B_POS[(_i * M + _j) * M + _k]] = 1.0

CORNERS = [(x, y, z) for x in (0, 1) for y in (0, 1) for z in (0, 1)]
PRIM = [(0, o) for o in CORNERS]
PRIM += [(1, (0, y, z)) for y in (0, 1) for z in (0, 1)]
PRIM += [(2, (x, 0, z)) for x in (0, 1) for z in (0, 1)]
PRIM += [(3, (x, y, 0)) for x in (0, 1) for y in (0, 1)]
S64 = one_hot([CORNERS.index(o) * 8 + t for t, o in PRIM], np.arange(20), (64, 24))
TILE = np.tile(np.eye(24, dtype=np.float32), (1, 8))
TMASK = (np.arange(64)[:, None] // 8 == np.arange(192)[None, :] // 24).astype(np.float32)
SPREAD = np.zeros((192, 128), np.float32)
for _c, _o1 in enumerate(CORNERS):
    for _q, (_t, _o2) in enumerate(PRIM):
        _f = [b - a + 1 for a, b in zip(_o1, _o2)]
        SPREAD[_c * 24 + _q, _t * 27 + (_f[0] * 3 + _f[1]) * 3 + _f[2]] = 1.0


def coarse_slots():
    m = np.arange(512)
    c, a, b, t = np.array(ORDER)[m // 64], m // 16 % 4, m // 4 % 4, m % 4
    da = (a[None, :] - a[:, None] + 1) % GX
    db = (b[None, :] - b[:, None] + 1) % GY
    dc = (c[None, :] - c[:, None] + 1) % GZ
    slot = t[None, :] * 27 + (da * 3 + db) * 3 + dc
    return np.where((da < 3) & (db < 3) & (dc < 3), slot, -1).astype(np.int32)


SLOTS = coarse_slots()


def dot(a, b, ca=1, cb=0):
    return lax.dot_general(
        a, b, (((ca,), (cb,)), ((), ())), precision=lax.Precision.HIGHEST, preferred_element_type=F32
    )


def pieces(x):
    h = x.astype(BF16)
    r = x - h.astype(F32)
    m = r.astype(BF16)
    return h, m, (r - m.astype(F32)).astype(BF16)


def pick(sel, x, ca=1, cb=0):
    out = None
    for p in pieces(x):
        d = lax.dot_general(sel, p, (((ca,), (cb,)), ((), ())), preferred_element_type=F32)
        out = d if out is None else out + d
    return out


def pick_cols(x, sel):
    out = None
    for p in pieces(x):
        d = lax.dot_general(p, sel, (((1,), (1,)), ((), ())), preferred_element_type=F32)
        out = d if out is None else out + d
    return out


def here():
    return lax.axis_index("gx"), lax.axis_index("gy"), lax.axis_index("gz")


def at(d):
    x, y, z = here()
    return (lax.rem(x + d[0] + GX, GX), lax.rem(y + d[1] + GY, GY), lax.rem(z + d[2] + GZ, GZ))


PLANE = [(x, y, 0) for x in range(GX) for y in range(GY) if (x, y) != (0, 0)]
LINE = [(0, 0, z) for z in range(1, GZ)]
_norm = lambda d: (d[0] % GX, d[1] % GY, d[2] % GZ)
PARTNERS = sorted({_norm(d) for d in DIRS + PLANE + LINE})


def barrier():
    sem = pltpu.get_barrier_semaphore()
    for d in PARTNERS:
        pl.semaphore_signal(sem, inc=1, device_id=at(d), device_id_type=MESH)
    pl.semaphore_wait(sem, len(PARTNERS))


def remote(src, dst, sems, k, d):
    return pltpu.make_async_remote_copy(
        src_ref=src, dst_ref=dst, send_sem=sems.at[2 * k], recv_sem=sems.at[2 * k + 1], device_id=at(d), device_id_type=MESH
    )


def exchange_start(send, recv, sems, k):
    for d in DIRS:
        o, n = OFFS[d]
        o2, _ = OFFS[tuple(-v for v in d)]
        remote(send.at[pl.ds(o, n)], recv.at[pl.ds(o2, n)], sems, k, d).start()


def bulk_wait(send, recv, sems, k):
    c = remote(send, recv, sems, k, (1, 0, 0))
    c.wait_recv()
    c.wait_send()


def owner_start(send, recv, sems, k):
    for c, o in enumerate(CORNERS):
        if c:
            remote(send.at[pl.ds(8 * c, 8)], recv.at[pl.ds(8 * c, 8)], sems, k, o).start()


def owner_finish(send, recv, sems, k):
    bulk_wait(send.at[pl.ds(8, 56)], recv.at[pl.ds(8, 56)], sems, k)
    out = send[pl.ds(0, 8), :]
    for c in range(1, 8):
        out = out + recv[pl.ds(8 * c, 8), :]
    return out


def gather_start(val, plane, sems, k):
    x, y, _ = here()
    ab = x * GY + y
    odd = lax.rem(y, 2) == 1
    plane[ab] = jnp.where(jnp.full((8, 128), odd), pltpu.roll(val, 4, 0), val)
    for d in PLANE:
        remote(plane.at[ab], plane.at[ab], sems, k, d).start()


def gather_turn(plane, full, sems, k):
    bulk_wait(plane.at[pl.ds(0, 15)], plane.at[pl.ds(0, 15)], sems, k)
    _, _, z = here()
    h = z // 2
    pos = lax.rem(z, 2) * h + (1 - lax.rem(z, 2)) * (6 - 2 * lax.rem(h, 2) + h // 2)
    rows = [plane[2 * i] + plane[2 * i + 1] for i in range(8)]
    mine = pl.ds(pl.multiple_of(pos * 64, 64), 64)
    full[mine, :] = jnp.concatenate(rows, axis=0)
    for d in LINE:
        remote(full.at[mine], full.at[mine], sems, k + 1, d).start()


def gather_finish(full, sems, k):
    bulk_wait(full.at[pl.ds(0, 448)], full.at[pl.ds(0, 448)], sems, k + 1)


def reduce_start(val, plane, sems, k):
    x, y, _ = here()
    ab = x * GY + y
    plane[ab] = val
    for d in PLANE:
        remote(plane.at[ab], plane.at[ab], sems, k, d).start()


def reduce_turn(plane, line, sems, k):
    bulk_wait(plane.at[pl.ds(0, 15)], plane.at[pl.ds(0, 15)], sems, k)
    _, _, z = here()
    line[z] = jnp.sum(plane[...], axis=0)
    for d in LINE:
        remote(line.at[z], line.at[z], sems, k + 1, d).start()


def reduce_finish(line, sems, k):
    bulk_wait(line.at[pl.ds(0, 7)], line.at[pl.ds(0, 7)], sems, k + 1)
    return jnp.sum(line[...], axis=0)


def prepare(load_ref, a_ref, di_ref, n_ref, phi_ref, pb_ref, pi_ref, s64_ref, tile_ref, tmask_ref, spread_ref,
            cl_ref, s_ref, nbb_ref, x_ref, p24_ref, start_ref, li_ref, k0_ref, k64_ref, flat):
    for i in range(M):
        for j in range(M):
            flat[pl.ds((i * M + j) * M, M), :] = load_ref[i, j]
    pb, pi = pb_ref[...], pi_ref[...]
    load = flat[...]
    lb, li = pick(pb, load), pick(pi, load)
    di = di_ref[...]
    start = dot(di, li)
    ab = pick(pb, a_ref[...])
    abb, abi = pick_cols(ab, pb), pick_cols(ab, pi)
    x = dot(di, abi, 1, 1)
    s = abb - dot(abi, x)
    cl_ref[:, 0:RHS] = lb - dot(abi, start)
    cl_ref[:, RHS : 2 * RHS] = lb
    s_ref[...] = s
    x_ref[...] = x
    start_ref[...] = start
    li_ref[...] = li
    k0_ref[...] = jnp.broadcast_to(jnp.sum(li * start, axis=0, keepdims=True), (8, RHS))
    nbb_ref[...] = pick_cols(pick(pb, n_ref[...]), pb)
    phi = pick_cols(phi_ref[...], pb)
    p24 = jnp.concatenate([phi, jnp.zeros((4, NB), F32)], axis=0)
    p24_ref[...] = p24
    k24 = dot(dot(p24, s), p24, 1, 1)
    k64 = dot(dot(s64_ref[...], k24), tile_ref[...]) * tmask_ref[...]
    k64_ref[...] = dot(k64, spread_ref[...])


def first(cl_ref, k64_ref, nbb_ref, p24_ref, pk_ref, wt_ref, s64_ref, asm_ref, w_ref, kall_ref, gall_ref,
          send, recv, ksend, krecv, hsend, hrecv, kplane, hplane, sems):
    barrier()
    ksend[...] = k64_ref[...]
    owner_start(ksend, krecv, sems, 0)
    pk = pk_ref[...]
    cl = cl_ref[...]
    send[...] = pick(pk, cl)
    exchange_start(send, recv, sems, 1)
    gather_start(owner_finish(ksend, krecv, sems, 0), kplane, sems, 2)
    bulk_wait(send, recv, sems, 1)
    asm = cl + pick(pk, recv[...], 0, 0)
    asm_ref[...] = asm
    f = wt_ref[...] * asm[:, 0:RHS]
    hsend[...] = dot(s64_ref[...], dot(p24_ref[...], f))
    owner_start(hsend, hrecv, sems, 4)
    gather_turn(kplane, kall_ref, sems, 2)
    w_ref[...] = dot(nbb_ref[...], f)
    gather_start(owner_finish(hsend, hrecv, sems, 4), hplane, sems, 5)
    gather_finish(kall_ref, sems, 2)
    gather_turn(hplane, gall_ref, sems, 5)
    gather_finish(gall_ref, sems, 5)


def sweep(ref, n, steps):
    lane = lax.broadcasted_iota(jnp.int32, (n, 128), 1)
    sub = lax.broadcasted_iota(jnp.int32, (n, 128), 0)
    base = lane // n * n

    def body(k, carry):
        idx = base + k
        for j in range(ref.shape[0]):
            x = ref[j]
            row = ref[j, pl.ds(k, 1), :]
            col = jnp.take_along_axis(x, idx, axis=1, mode="promise_in_bounds")
            piv = jnp.take_along_axis(jnp.broadcast_to(row, (8, 128)), idx[0:8], axis=1, mode="promise_in_bounds")[0:1]
            inv = 1.0 / piv
            scaled = row * inv
            oncol = lane == idx
            new = jnp.where(oncol, -col * inv, x - col * scaled)
            ref[j] = jnp.where(sub == k, jnp.where(oncol, inv, scaled), new)
        return carry

    lax.fori_loop(0, steps, body, 0)


def coarse(kall_ref, slots_ref, w24_ref, kc, xo, x2, xf):
    kall = kall_ref[...]
    for j in range(4):
        cut = pl.ds(128 * j, 128)
        idx = slots_ref[:, cut]
        v = jnp.take_along_axis(kall, jnp.maximum(idx, 0), axis=1, mode="promise_in_bounds")
        kc[:, cut] = jnp.where(idx >= 0, v, 0.0)
    low = lax.broadcasted_iota(jnp.int32, (64, 128), 1) < 64
    for j in range(2):
        cut = pl.ds(128 * j, 128)
        xo[j] = jnp.where(low, kc[pl.ds(128 * j, 64), cut], kc[pl.ds(128 * j + 64, 64), cut])
    sweep(xo, 64, 64)
    group = lax.broadcasted_iota(jnp.int32, (64, 256), 1) // 64
    both = jnp.concatenate([xo[0], xo[1]], axis=1)
    inv_o = jnp.concatenate([jnp.where(group == g, both, 0.0) for g in range(4)], axis=0)
    koe = kc[pl.ds(0, 256), pl.ds(256, 256)]
    m = dot(inv_o, koe)
    se = kc[pl.ds(256, 256), pl.ds(256, 256)] - dot(koe, m, 0, 0)
    x2[0] = jnp.where(low, se[0:64, 0:128], se[64:128, 0:128])
    sweep(x2, 64, 64)
    inv_2 = jnp.concatenate([jnp.where(low, x2[0], 0.0), jnp.where(low, 0.0, x2[0])], axis=0)
    k2f = se[0:128, 128:256]
    m2 = dot(inv_2, k2f)
    xf[0] = se[128:256, 128:256] - dot(k2f, m2, 0, 0)
    sweep(xf, 128, 128)
    x, y, z = here()
    p = lax.broadcasted_iota(jnp.int32, (24, 512), 0)
    col = lax.broadcasted_iota(jnp.int32, (24, 512), 1)
    want = jnp.full((24, 512), -1, jnp.int32)
    for q, (t, o) in enumerate(PRIM):
        cx, cy, cz = at(o)
        h = cz // 2
        pos = lax.rem(cz, 2) * h + (1 - lax.rem(cz, 2)) * (6 - 2 * lax.rem(h, 2) + h // 2)
        want = jnp.where(p == q, pos * 64 + (cx * GY + cy) * 4 + t, want)
    sel = (want == col).astype(F32)
    so = sel[:, 0:256]
    s_e = sel[:, 256:512] - dot(so, m)
    s_2 = s_e[:, 0:128]
    wf = dot(s_e[:, 128:256] - dot(s_2, m2), xf[0])
    w2 = dot(s_2, inv_2) - dot(wf, m2, 1, 1)
    we = jnp.concatenate([w2, wf], axis=1)
    w24_ref[:, 256:512] = we
    w24_ref[:, 0:256] = dot(so, inv_o) - dot(we, m, 1, 1)


def second(cl_ref, asm_ref, w_ref, gall_ref, w24_ref, s_ref, nbb_ref, p24_ref, k0_ref, pk_ref, wt_ref, s64_ref,
           z1_ref, z2_ref, at1_ref, at2_ref, sums_ref,
           send, recv, hsend, hrecv, hplane, gfull, rplane, rline, sems):
    barrier()
    pk, wt, p24 = pk_ref[...], wt_ref[...], p24_ref[...]
    c = cl_ref[:, 0:RHS]
    s = s_ref[...]

    def swap_start(k, v):
        send[k] = pick(pk, v)
        exchange_start(send.at[k], recv.at[k], sems, k)

    def swap_finish(k, v):
        bulk_wait(send.at[k], recv.at[k], sems, k)
        return v + pick(pk, recv[k], 0, 0)

    def apply_coarse(w, g):
        y = dot(w24_ref[...], g)
        return wt * (w + dot(p24, y, 0, 0))

    u = apply_coarse(w_ref[...], gall_ref[...])
    swap_start(0, u)
    z1 = swap_finish(0, u)
    t1 = dot(s, z1)
    swap_start(1, t1)
    z1_ref[...] = z1
    k0 = k0_ref[...]
    part = lambda a, b: jnp.sum(a * b, axis=0, keepdims=True)
    zero = jnp.zeros((5, RHS), F32)
    reduce_start(jnp.concatenate([k0[0:1], part(c, z1), part(z1, t1), zero], axis=0), rplane.at[0], sems, 4)
    at1 = swap_finish(1, t1)
    at1_ref[...] = at1
    f = wt * at1
    hsend[...] = dot(s64_ref[...], dot(p24, f))
    owner_start(hsend, hrecv, sems, 6)
    w = dot(nbb_ref[...], f)
    reduce_turn(rplane.at[0], rline.at[0], sems, 4)
    gather_start(owner_finish(hsend, hrecv, sems, 6), hplane, sems, 7)
    gather_turn(hplane, gfull, sems, 7)
    sums = reduce_finish(rline.at[0], sems, 4)
    k0s = sums[0:1]
    g0 = k0s + sums[1:2]
    s1 = g0 / (k0s + sums[2:3])
    gather_finish(gfull, sems, 7)
    u = apply_coarse(w, gfull[...])
    swap_start(2, u)
    z2 = swap_finish(2, u)
    t2 = dot(s, z2)
    swap_start(3, t2)
    z2_ref[...] = z2
    zp, tp, cp = z1 - s1 * z2, t1 - s1 * t2, c - s1 * t1
    zero = jnp.zeros((6, RHS), F32)
    reduce_start(jnp.concatenate([part(cp, zp), part(zp, tp), zero], axis=0), rplane.at[1], sems, 9)
    at2_ref[...] = swap_finish(3, t2)
    reduce_turn(rplane.at[1], rline.at[1], sems, 9)
    last = reduce_finish(rline.at[1], sems, 9)
    rest = 1.0 - s1
    g1 = rest * rest * k0s + last[0:1]
    beta = g1 / g0
    s2 = g1 / (rest * rest * k0s + last[1:2] - beta * g1 / s1)
    sums_ref[...] = jnp.concatenate([s1, beta, s2, jnp.zeros((5, RHS), F32)], axis=0)


def finish(sums_ref, z1_ref, z2_ref, at1_ref, at2_ref, asm_ref, x_ref, start_ref, li_ref, pb_ref, pi_ref, sol_ref, res_ref, flat):
    s1, beta, s2 = sums_ref[0:1, :], sums_ref[1:2, :], sums_ref[2:3, :]
    rest = 1.0 - s1
    z1, at1 = z1_ref[...], at1_ref[...]
    xb = s1 * z1 + s2 * ((z1 - s1 * z2_ref[...]) + beta * z1)
    xi = (s1 + s2 * (rest + beta)) * start_ref[...] - dot(x_ref[...], xb)
    kappa = rest * (1.0 - s2) - s2 * beta
    ac = asm_ref[:, 0:RHS]
    ae = asm_ref[:, RHS : 2 * RHS] - ac
    rb = kappa * ae + (ac - s1 * at1) - s2 * ((at1 - s1 * at2_ref[...]) + beta * at1)
    ri = kappa * li_ref[...]
    pb, pi = pb_ref[...], pi_ref[...]
    both = pick(pb, jnp.concatenate([xb, rb], axis=1), 0, 0) + pick(pi, jnp.concatenate([xi, ri], axis=1), 0, 0)
    flat[...] = both
    for i in range(M):
        for j in range(M):
            rows = pl.ds((i * M + j) * M, M)
            sol_ref[i, j] = flat[rows, 0:RHS]
            res_ref[i, j] = flat[rows, RHS : 2 * RHS]


def call(kernel, out_shapes, scratch=(), collective=None):
    params = dict(vmem_limit_bytes=60 * 2**20)
    if collective is not None:
        params |= dict(collective_id=collective, has_side_effects=True)
    outs = [jax.ShapeDtypeStruct(s, F32) for s in out_shapes]

    def run(*args):
        return pl.pallas_call(
            kernel, out_shape=outs, in_specs=[VM] * len(args), out_specs=[VM] * len(outs),
            scratch_shapes=list(scratch), compiler_params=pltpu.CompilerParams(**params), name=kernel.__name__,
        )(*args)

    return run


def local(load, a, di, n, phi):
    a, n = a.reshape(NODES, NODES), n.reshape(NODES, NODES)
    di, phi = di.reshape(NI, NI), phi.reshape(20, NODES)
    pb, pi, pk = (jnp.asarray(v, BF16) for v in (PB, PI, PK))
    wt, s64 = jnp.asarray(WEIGHT), jnp.asarray(S64)
    V = lambda *s: pltpu.VMEM(s, F32)
    cl, s, nbb, x, p24, start, li, k0, k64 = call(
        prepare,
        [(NB, 2 * RHS), (NB, NB), (NB, NB), (NI, NB), (24, NB), (NI, RHS), (NI, RHS), (8, RHS), (64, 128)],
        [V(NODES, RHS)],
    )(load, a, di, n, phi, pb, pi, s64, jnp.asarray(TILE), jnp.asarray(TMASK), jnp.asarray(SPREAD))
    asm, w, kall, gall = call(
        first,
        [(NB, 2 * RHS), (NB, RHS), (512, 128), (512, 128)],
        [V(NS, 2 * RHS), V(NS, 2 * RHS), V(64, 128), V(64, 128), V(64, 128), V(64, 128), V(16, 8, 128), V(16, 8, 128),
         pltpu.SemaphoreType.DMA((14,))],
        0,
    )(cl, k64, nbb, p24, pk, wt, s64)
    (w24,) = call(coarse, [(24, 512)], [V(512, 512), V(2, 64, 128), V(1, 64, 128), V(1, 128, 128)])(kall, jnp.asarray(SLOTS))
    z1, z2, at1, at2, sums = call(
        second,
        [(NB, RHS)] * 4 + [(8, RHS)],
        [V(4, NS, RHS), V(4, NS, RHS), V(64, 128), V(64, 128), V(16, 8, 128), V(512, 128), V(2, 16, 8, 128), V(2, 8, 8, 128),
         pltpu.SemaphoreType.DMA((22,))],
        1,
    )(cl, asm, w, gall, w24, s, nbb, p24, k0, pk, wt, s64)
    return tuple(
        call(finish, [(M, M, M, RHS)] * 2, [V(NODES, 2 * RHS)])(sums, z1, z2, at1, at2, asm, x, start, li, pb, pi)
    )


def solution(mesh):
    spec4, spec5 = P("gx", "gy", "gz", None), P("gx", "gy", "gz", None, None)
    return jax.shard_map(
        local, mesh=mesh, in_specs=(spec4, spec5, spec5, spec5, spec5), out_specs=(spec4, spec4), check_vma=False
    )
```

time: 607 us -> 167 us (0.28)
  other arithmetic: 161 us -> 0 us
  Pallas kernels: 0 us -> 158 us
  blocking collectives: 108 us -> 0 us
  waiting for transfers between devices: 101 us -> 0 us
  matrix products: 76 us -> 0 us
  local copies, waits for them, and re-layouts: 74.1 us -> 7.97 us
  starting transfers between devices: 62.3 us -> 0 us
  between operations: 18.4 us -> 0.65 us
    pallas_call x0 -> x5, Pallas kernels: none -> 158 us  [run(): pl.pallas_call(kernel, out_shape=outs, in_specs=[VM] * len(args), out_spe...]
    another operation x19 -> x0, other arithmetic: 128 us -> none  [the longest x15 86.6 us: local(): factor = jnp.linalg.cholesky(coarse_matrix)]
    psum x8 -> x0, blocking collectives: 68.1 us -> none  [over_axes(): return functools.reduce(lax.psum, axes, array)]
    all_gather x2 -> x0, waiting for transfers between devices: 65.6 us -> none  [coarse_rhs(): received = lax.all_gather(primal_load[None], GX_GY_GZ, axis=0, tiled=True)]
    ppermute x42 -> x0, starting transfers between devices: 61.8 us -> none  [the longest x21 39.1 us: with_halo(): after = lax.ppermute(leading, axis, down)]
    dot_general x24 -> x0, matrix products: 59.9 us -> none  [the longest x20 36.9 us: matmul(): jnp.dot(left_side, right_side, precision=lax.Precision.HIGHEST, preferred...]
    all_gather x1 -> x0, blocking collectives: 40.2 us -> none  [local(): received = lax.all_gather(coarse_local[None], GX_GY_GZ, axis=0, tiled=True)]
    ppermute x42 -> x0, waiting for transfers between devices: 35.7 us -> none  [the longest x21 21.6 us: with_halo(): before = lax.ppermute(last, axis, up)]
  transfers between devices with their start and end apart: 44 -> 0, of which waited for: 26 -> 0; matrix products, arithmetic and copies ran while one was open for 36% -> 0% of each run, Pallas kernels for 0% -> 0%
where the time goes in v1:
time: 167 us
  Pallas kernels  158 us (95%)
  local copies, waits for them, and re-layouts  7.97 us (5%)
    pallas_call x5, Pallas kernels, run(): pl.pallas_call(kernel, out_shape=outs, in_specs=[VM] * len(args), out_spe...  158 us
    unnamed x3, local copies, waits for them, and re-layouts  7.97 us

profile of v1, /device:TPU:1, one launch (start us, length us, event | category | flops | bytes accessed | tf_op | source)
XLA Modules:
  0.0 166.6 jit_solution(12636104102822246007)
XLA Ops:
  0.6 1.5 copy.25
  2.1 1.9 %copy.24 = f32[1,1,1,343,343]{4,3,2,1,0:T(8,128)} copy(f32[1,1,1,343,343]{4,2,3,1,0:T(1,128)} %param.16) | data formatting | bytes 941192
  4.0 4.6 %copy_bitcast_fusion = (f32[729,729]{1,0:T(8,128)}, f32[729,729]{1,0:T(8,128)}) fusion(f32[1,1,1,729,729]{4,2,3,1,0:T(1,128)} %param.17, f32[1,1,1,729,729]{4,2,3,1,0:T(1,128)} %param.15), kind=kLoop, calls=%fused_computation | loop fusion | bytes 8503056
  8.6 18.9 %prepare.1 = (f32[392,256]{1,0:T(8,128)}, f32[392,392]{1,0:T(8,128)}, f32[392,392]{1,0:T(8,128)}, f32[343,392]{1,0:T(8,128)}, f32[24,392]{1,0:T(8,128)}, /*index...) custom-call(f32[9,9,9,128]{3,2,1,0:T(8,128)} %load_ref.1, ...), custom_call_target="tpu_custom_call" | custom-call | tf_op jit(solution)/shard_map/prepare/pallas_call | solution.py:423
  27.5 34.7 %first.1 = (f32[392,256]{1,0:T(8,128)}, f32[392,128]{1,0:T(8,128)}, f32[512,128]{1,0:T(8,128)}, f32[512,128]{1,0:T(8,128)}) custom-call(f32[392,256]{1,0:T(8,128)} %get-tuple-element.20.cl_ref, f32[64,128]{1,0:T(8,128)} %get-tuple-element.21.k64_ref, f32[392,392]{1,0:T(8,128)} %get-tuple-element.22.nbb_ref, f32[24,392]{1,0:T(8,128)} %get-tuple-element.23.p24_ref, ...), custom_call_target="tpu_custom_call" | custom-call | tf_op jit(solution)/shard_map/first/pallas_call | solution.py:423
  62.2 35.4 %coarse.1.w24_ref = f32[24,512]{1,0:T(8,128)} custom-call(f32[512,128]{1,0:T(8,128)} %get-tuple-element.27.kall_ref, s32[512,512]{1,0:T(8,128)} %constant.26.clone.slots_ref), custom_call_target="tpu_custom_call" | custom-call | tf_op jit(solution)/shard_map/coarse/pallas_call | solution.py:423
  97.6 63.3 %second.1 = (f32[392,128]{1,0:T(8,128)}, f32[392,128]{1,0:T(8,128)}, f32[392,128]{1,0:T(8,128)}, f32[392,128]{1,0:T(8,128)}, f32[8,128]{1,0:T(8,128)}) custom-call(f32[392,256]{1,0:T(8,128)} %get-tuple-element.20.cl_ref, f32[392,256]{1,0:T(8,128)} %get-tuple-element.24.asm_ref, f32[392,128]{1,0:T(8,128)} %get-tuple-element.25.w_ref, ...), custom_call_target="tpu_custom_call" | custom-call | tf_op jit(solution)/shard_map/second/pallas_call | solution.py:423
  160.9 5.7 %finish.1 = (f32[9,9,9,128]{3,2,1,0:T(8,128)}, f32[9,9,9,128]{3,2,1,0:T(8,128)}) custom-call(f32[8,128]{1,0:T(8,128)} %get-tuple-element.30.sums_ref, f32[392,128]{1,0:T(8,128)} %get-tuple-element.31.z1_ref, f32[392,128]{1,0:T(8,128)} %get-tuple-element.32.z2_ref, f32[392,128]{1,0:T(8,128)} %get-tuple-element.33.at1_ref, ...), custom_call_target="tpu_custom_call" | custom-call | tf_op jit(solution)/shard_map/finish/pallas_call | solution.py:423
